TPU v7x, 256 devices: a whole 4x4x8 slice. The times are simulated.
256 devices in a mesh: tok: 16 (over y, x), col: 16 (over z, core).
Axes of the slice: x: 4, y: 4, z: 8, core: 2. Of those that a mesh axis runs over, the one named last changes fastest.
Arguments:
- activations: bfloat16 [32768, 8192], P('tok', 'col'), may hold values from -60 to 60, as said below
- weight: bfloat16 [8192, 8192], P('tok', 'col'), may hold values from -6 to 6
- keep_mask: int32 [8192, 8192], P('tok', 'col'), may hold values from 0 to 1
Outputs:
- new_weight: bfloat16 [8192, 8192], P('tok', 'col')
Inputs may be any that keep to these rules, and one draw needn't show every extreme that they name: activations of calibration tokens.
All inputs are finite; a program needn't handle non-finite values.
Results may differ from a plain program's by a relative error of at most 0.00115.
Values may be sent and summed in bfloat16 or wider, within the bound.
A program may use at most 64 MiB of HBM per device.

v0:
```python
import jax
import jax.numpy as jnp
from jax import lax
from jax.sharding import PartitionSpec as P

B = 1024
ITERS = 4


def per_device(activations, weight, keep_mask):
    highest = lax.Precision.HIGHEST
    n_col = lax.axis_size("col")
    n_tok = lax.axis_size("tok")
    tok_rows = activations.shape[0]
    panel_width = B // n_col
    total_count = tok_rows * n_tok
    partial_panel = lax.dot_general(
        activations,
        lax.all_gather(activations[:, :panel_width], "col", axis=1, tiled=True),
        (((0,), (0,)), ((), ())),
        preferred_element_type=jnp.float32,
    )
    hessian_panel = lax.psum(partial_panel, "tok") / total_count
    block_part = hessian_panel[:panel_width]
    diagonal_block = lax.all_gather(block_part, "col", axis=0, tiled=True)
    identity = jnp.eye(B, dtype=jnp.float32)
    damping = 0.01 * jnp.mean(jnp.diagonal(diagonal_block))
    damped = diagonal_block + damping * identity
    frobenius = jnp.sqrt(jnp.sum(damped * damped))
    col_index = lax.axis_index("col")
    row_ids = col_index * panel_width + lax.iota(jnp.int32, panel_width)
    iterate = (row_ids[:, None] == lax.iota(jnp.int32, B)[None, :]).astype(jnp.float32) / frobenius
    for sweep in range(ITERS):
        if sweep == 0:
            whole = identity / frobenius
        else:
            whole = lax.all_gather(iterate.astype(jnp.bfloat16), "col", axis=0, tiled=True).astype(
                iterate.dtype
            )
        product = jnp.dot(iterate, damped, precision=highest)
        iterate = 2.0 * iterate - jnp.dot(product, whole, precision=highest)
    inverse = lax.all_gather(iterate, "col", axis=0, tiled=True)
    pruned = jnp.where(
        keep_mask[:, :panel_width] == 0, weight[:, :panel_width], jnp.zeros((), jnp.bfloat16)
    )
    pruned_panel = lax.all_gather(pruned, "col", axis=1, tiled=True).astype(jnp.float32)
    factor_rows = jnp.dot(pruned_panel, inverse, precision=highest)
    correction = lax.dot_general(
        factor_rows, hessian_panel, (((1,), (1,)), ((), ())), precision=highest
    )
    kept = keep_mask.astype(jnp.float32)
    return (kept * (weight.astype(jnp.float32) - correction)).astype(jnp.bfloat16)


def solution(mesh):
    return jax.shard_map(
        per_device,
        mesh=mesh,
        in_specs=(P("tok", "col"), P("tok", "col"), P("tok", "col")),
        out_specs=P("tok", "col"),
        check_vma=False,
    )
```

profile of v0, /device:TPU:1, one launch (start us, length us, event | category | flops | bytes accessed | tf_op | source)
XLA Modules:
  0.0 456.3 jit_solution(11155648659330884020)
XLA Ops:
  6.5 1.1 slice.14
  7.6 0.9 copy.9
  8.6 47.0 %all-gather.10.cloned.1.call-done = bf16[2048,1024]{0,1:T(8,128)(2,1)} async-done(((bf16[2048,64]{0,1:T(8,128)(2,1)}), bf16[2048,1024]{0,1:T(8,128)(2,1)}) %all-gather.10.cloned.1.call-update) | async-done | bytes 4194320 | tf_op jit(solution)/shard_map/all_gather | solution.py:19
  55.5 6.6 %fusion.25 = f32[512,1024]{1,0:T(8,128)} fusion(bf16[2048,512]{1,0:T(8,128)(2,1)} %param.3, bf16[2048,1024]{0,1:T(8,128)(2,1)} %all-gather.10.cloned.1.call-done), kind=kOutput, calls=%fused_computation.37 | convolution fusion | flops 2147483648 | bytes 8388608 | tf_op jit(solution)/shard_map/dot_general | solution.py:17
  62.2 97.5 %all-reduce.2.cloned.1.call-done = f32[512,1024]{1,0:T(8,128)} async-done(((f32[512,1024]{1,0:T(8,128)}), f32[512,1024]{1,0:T(8,128)}) %all-reduce.2.cloned.1.call-update) | async-done | bytes 2097168 | tf_op jit(solution)/shard_map/psum | solution.py:23
  159.7 1.8 broadcast_multiply_fusion
  162.3 43.1 %all-gather.12.cloned.1.call-done = f32[1024,1024]{1,0:T(8,128)} async-done(((f32[64,1024]{1,0:T(8,128)}), f32[1024,1024]{1,0:T(8,128)}) %all-gather.12.cloned.1.call-update) | async-done | bytes 4194320 | tf_op jit(solution)/shard_map/all_gather | solution.py:25
  205.5 17.2 %gather_fusion = f32[1024]{0:T(1024)S(1)} fusion(f32[1024,1024]{1,0:T(8,128)} %all-gather.12.cloned.1.call-done, s32[1024]{0:T(1024)S(1)} %bitcast.16), kind=kCustom, calls=%fused_computation | custom fusion | bytes 16384 | tf_op jit(solution)/shard_map/jit(diagonal)/cond/branch_0_fun/gather | solution.py:27
  223.9 3.9 multiply_reduce_fusion
  228.5 4.9 %fusion.9 = f32[64,1024]{1,0:T(8,128)S(1)} fusion(f32[1024,1024]{1,0:T(8,128)} %all-gather.12.cloned.1.call-done, f32[]{:T(128)S(6)} %mul_shard_map.3, f32[]{:T(128)S(6)} %sqrt.3, s32[64]{0:T(128)S(1)} %iota_add_fusion), kind=kOutput, calls=%fused_computation.14 | convolution fusion | flops 808583168 | bytes 4456712 | tf_op jit(solution)/shard_map/dot_general | solution.py:40
  233.4 1.9 fusion.22
  235.4 4.9 %fusion.8 = f32[64,1024]{1,0:T(8,128)S(1)} fusion(f32[64,1024]{1,0:T(8,128)S(1)} %get-tuple-element.6, f32[1024,1024]{1,0:T(8,128)} %all-gather.12.cloned.1.call-done, f32[]{:T(128)S(6)} %mul_shard_map.3), kind=kOutput, calls=%fused_computation.13 | convolution fusion | flops 808452096 | bytes 4718596 | tf_op jit(solution)/shard_map/dot_general | solution.py:40
  240.3 33.5 %all-gather.14.cloned.1.call-done = bf16[1024,1024]{1,0:T(8,128)(2,1)} async-done(((bf16[64,1024]{1,0:T(8,128)(2,1)}), bf16[1024,1024]{1,0:T(8,128)(2,1)}) %all-gather.14.cloned.1.call-update) | async-done | bytes 2097168 | tf_op jit(solution)/shard_map/all_gather | solution.py:37
  273.8 3.5 fusion.23
  277.5 4.9 %fusion.7 = f32[64,1024]{1,0:T(8,128)S(1)} fusion(f32[64,1024]{1,0:T(8,128)S(1)} %get-tuple-element.8, f32[1024,1024]{1,0:T(8,128)} %all-gather.12.cloned.1.call-done, f32[]{:T(128)S(6)} %mul_shard_map.3), kind=kOutput, calls=%fused_computation.12 | convolution fusion | flops 808452096 | bytes 4718596 | tf_op jit(solution)/shard_map/dot_general | solution.py:40
  282.5 33.0 %all-gather.16.cloned.1.call-done = bf16[1024,1024]{1,0:T(8,128)(2,1)} async-done(((bf16[64,1024]{1,0:T(8,128)(2,1)}), bf16[1024,1024]{1,0:T(8,128)(2,1)}) %all-gather.16.cloned.1.call-update) | async-done | bytes 2097168 | tf_op jit(solution)/shard_map/all_gather | solution.py:37
  315.5 3.5 fusion.24
  320.0 4.9 %fusion.6 = f32[64,1024]{1,0:T(8,128)S(1)} fusion(f32[64,1024]{1,0:T(8,128)S(1)} %get-tuple-element.10, f32[1024,1024]{1,0:T(8,128)} %all-gather.12.cloned.1.call-done, f32[]{:T(128)S(6)} %mul_shard_map.3), kind=kOutput, calls=%fused_computation.11 | convolution fusion | flops 808452096 | bytes 4718596 | tf_op jit(solution)/shard_map/dot_general | solution.py:40
  324.9 32.3 %all-gather.18.cloned.1.call-done = bf16[1024,1024]{1,0:T(8,128)(2,1)} async-done(((bf16[64,1024]{1,0:T(8,128)(2,1)}), bf16[1024,1024]{1,0:T(8,128)(2,1)}) %all-gather.18.cloned.1.call-update) | async-done | bytes 2097168 | tf_op jit(solution)/shard_map/all_gather | solution.py:37
  357.2 3.5 convolution_subtract_fusion.1
  360.7 35.4 %all-gather.8.cloned.1.call-done = bf16[512,1024]{0,1:T(8,128)(2,1)} async-done(((bf16[512,64]{0,1:T(8,128)(2,1)}), bf16[512,1024]{0,1:T(8,128)(2,1)}) %all-gather.8.cloned.1.call-update) | async-done | bytes 1048592 | tf_op jit(solution)/shard_map/all_gather | solution.py:46
  396.1 42.8 %all-gather.20.cloned.1.call-done = f32[1024,1024]{1,0:T(8,128)} async-done(((f32[64,1024]{1,0:T(8,128)}), f32[1024,1024]{1,0:T(8,128)}) %all-gather.20.cloned.1.call-update) | async-done | bytes 4194320 | tf_op jit(solution)/shard_map/all_gather | solution.py:42
  438.9 6.1 %fusion.26 = f32[512,1024]{1,0:T(8,128)S(1)} fusion(bf16[512,1024]{0,1:T(8,128)(2,1)} %all-gather.8.cloned.1.call-done, f32[1024,1024]{1,0:T(8,128)} %all-gather.20.cloned.1.call-done), kind=kOutput, calls=%fused_computation.38 | convolution fusion | flops 6442450944 | bytes 7340032 | tf_op jit(solution)/shard_map/dot_general | solution.py:47
  445.0 4.5 fusion.5
  (33 shorter events, 2.8 us)
Async XLA Ops:
  6.5 49.0 %all-gather.10.cloned.1.call-start = ((), (), s32[]{:S(2)}) async-start(), calls=%async_computation.1 | async-start | bytes 4456448 | tf_op jit(solution)/shard_map/all_gather | solution.py:19
  8.5 151.2 %all-reduce.2.cloned.1.call-start = ((), (), s32[]{:S(2)}) async-start(), calls=%async_computation.2 | async-start | bytes 4194304 | tf_op jit(solution)/shard_map/psum | solution.py:23
  62.2 143.3 %all-gather.12.cloned.1.call-start = ((), (), s32[]{:S(2)}) async-start(), calls=%async_computation.3 | async-start | bytes 4456448 | tf_op jit(solution)/shard_map/all_gather | solution.py:25
  162.3 111.5 %all-gather.14.cloned.1.call-start = ((), (), s32[]{:S(2)}) async-start(), calls=%async_computation.4 | async-start | bytes 2228224 | tf_op jit(solution)/shard_map/all_gather | solution.py:37
  235.3 80.1 %all-gather.16.cloned.1.call-start = ((), (), s32[]{:S(2)}) async-start(), calls=%async_computation.5 | async-start | bytes 2228224 | tf_op jit(solution)/shard_map/all_gather | solution.py:37
  277.3 79.9 %all-gather.18.cloned.1.call-start = ((), (), s32[]{:S(2)}) async-start(), calls=%async_computation.6 | async-start | bytes 2228224 | tf_op jit(solution)/shard_map/all_gather | solution.py:37
  277.5 41.5 %slice-start = ((s32[512,512]{1,0:T(8,128)}), s32[512,64]{1,0:T(8,128)S(1)}, s32[]{:S(2)}) async-start(s32[512,512]{1,0:T(8,128)} %param.5), calls=%async_computation.8 | async-start | bytes 524288 | tf_op jit(solution)/shard_map/slice | solution.py:44
  277.5 41.6 %slice-start.1 = ((bf16[512,512]{1,0:T(8,128)(2,1)}), bf16[512,64]{1,0:T(8,128)(2,1)S(1)}, s32[]{:S(2)}) async-start(bf16[512,512]{1,0:T(8,128)(2,1)} %param.4), calls=%async_computation.9 | async-start | bytes 262144 | tf_op jit(solution)/shard_map/slice | solution.py:44
  319.0 77.2 %all-gather.8.cloned.1.call-start = ((), (), s32[]{:S(2)}) async-start(), calls=%async_computation | async-start | bytes 1114112 | tf_op jit(solution)/shard_map/all_gather | solution.py:46
  319.9 119.0 %all-gather.20.cloned.1.call-start = ((), (), s32[]{:S(2)}) async-start(), calls=%async_computation.7 | async-start | bytes 4456448 | tf_op jit(solution)/shard_map/all_gather | solution.py:42
  360.7 84.3 %copy-start = (f32[512,1024]{1,0:T(8,128)S(1)}, f32[512,1024]{1,0:T(8,128)}, u32[]{:S(2)}) copy-start(f32[512,1024]{1,0:T(8,128)} %all-reduce.2.cloned.1.call-done) | copy-start | bytes 6291460
  360.7 84.3 %copy-start.1 = (s32[512,512]{1,0:T(8,128)S(1)}, s32[512,512]{1,0:T(8,128)}, u32[]{:S(2)}) copy-start(s32[512,512]{1,0:T(8,128)} %param.5) | copy-start | bytes 3145732
  438.9 6.1 %copy-start.2 = (bf16[512,512]{1,0:T(8,128)(2,1)S(1)}, bf16[512,512]{1,0:T(8,128)(2,1)}, u32[]{:S(2)}) copy-start(bf16[512,512]{1,0:T(8,128)(2,1)} %param.4) | copy-start | bytes 1572868
Sparse Core Ops, SparseCore 0:
  9.2 46.3 all-gather.9
  62.3 97.4 all-reduce.1
  162.4 43.0 all-gather.11
  235.5 38.2 all-gather.13
  277.4 38.0 all-gather.15
  319.1 38.0 all-gather.17
  359.1 36.9 all-gather.7
  398.1 40.7 all-gather.19
where the time goes:
time: 457 us; the launch traced here: 456 us
  waiting for transfers between devices  365 us (80%)
  matrix products  49.1 us (11%)
  local copies, waits for them, and re-layouts  20.1 us (4%)
  between operations  15 us (3%)
  other arithmetic  6.89 us (2%)
    all_gather x3, waiting for transfers between devices, per_device(): lax.all_gather(iterate.astype(jnp.bfloat16), 'col', axis=0, tiled=True)  98.8 us
    psum x1, waiting for transfers between devices, per_device(): hessian_panel = lax.psum(partial_panel, 'tok') / total_count  97.5 us
    all_gather x1, waiting for transfers between devices, per_device(): lax.all_gather(activations[:, :panel_width], 'col', axis=1, tiled=True)  47 us
    all_gather x1, waiting for transfers between devices, per_device(): diagonal_block = lax.all_gather(block_part, 'col', axis=0, tiled=True)  43.1 us
    all_gather x1, waiting for transfers between devices, per_device(): inverse = lax.all_gather(iterate, 'col', axis=0, tiled=True)  42.8 us
    all_gather x1, waiting for transfers between devices, per_device(): lax.all_gather(pruned, 'col', axis=1, tiled=True).astype(jnp.float32)  35.4 us
    dot_general x4, matrix products, per_device(): product = jnp.dot(iterate, damped, precision=highest)  19.6 us
    gather x1, local copies, waits for them, and re-layouts, per_device(): damping = 0.01 * jnp.mean(jnp.diagonal(diagonal_block))  17.2 us
  transfers between devices with their start and end apart: 8, of which 8 were waited for; matrix products, arithmetic and copies ran while one was open for 4% of the time, Pallas kernels for 0%

commit v1 on v0

--- a/solution.py
+++ b/solution.py
@@ -39,7 +39,21 @@
             )
         product = jnp.dot(iterate, damped, precision=highest)
         iterate = 2.0 * iterate - jnp.dot(product, whole, precision=highest)
-    inverse = lax.all_gather(iterate, "col", axis=0, tiled=True)
+    ways, here, step = (lax.axis_size("col"), lax.axis_index("col"), iterate.shape[0])
+    dims = [n * ways if d == 0 else n for d, n in enumerate(iterate.shape)]
+    full = lax.dynamic_update_slice_in_dim(
+        jnp.zeros(dims, iterate.dtype), iterate, here * step, axis=0
+    )
+    going_up = going_down = iterate
+    for far in range(1, ways // 2 + 1):
+        going_up = lax.ppermute(going_up, "col", [(d, (d + 1) % ways) for d in range(ways)])
+        full = lax.dynamic_update_slice_in_dim(full, going_up, (here - far) % ways * step, axis=0)
+        if 2 * far < ways:
+            going_down = lax.ppermute(going_down, "col", [(d, (d - 1) % ways) for d in range(ways)])
+            full = lax.dynamic_update_slice_in_dim(
+                full, going_down, (here + far) % ways * step, axis=0
+            )
+    inverse = full
     pruned = jnp.where(
         keep_mask[:, :panel_width] == 0, weight[:, :panel_width], jnp.zeros((), jnp.bfloat16)
     )

time: 457 us -> 437 us (0.956)
  waiting for transfers between devices: 365 us -> 298 us
  starting transfers between devices: 0.48 us -> 30.5 us
  local copies, waits for them, and re-layouts: 20.1 us -> 33.9 us
    all_gather x1 -> x0, waiting for transfers between devices: 42.8 us -> none  [per_device(): inverse = lax.all_gather(iterate, 'col', axis=0, tiled=True)]
    all_gather x1, waiting for transfers between devices: 35.4 us -> 0.01 us  [per_device(): lax.all_gather(pruned, 'col', axis=1, tiled=True).astype(jnp.float32)]
    ppermute x0 -> x15, starting transfers between devices: none -> 30.1 us  [the longest x7 20.8 us: per_device(): lax.ppermute(going_down, 'col', [(d, (d - 1) % ways) for d in range(ways)])]
    ppermute x0 -> x15, waiting for transfers between devices: none -> 10.8 us  [the longest x8 10.1 us: per_device(): lax.ppermute(going_up, 'col', [(d, (d + 1) % ways) for d in range(ways)])]
    dynamic_update_slice x0 -> x15, local copies, waits for them, and re-layouts: none -> 10.8 us  [the longest x8 5.74 us: per_device(): lax.dynamic_update_slice_in_dim(full, going_up, (here - far) % ways * ste...]
  transfers between devices with their start and end apart: 8 -> 22, of which waited for: 8 -> 13; matrix products, arithmetic and copies ran while one was open for 4% -> 6% of each run, Pallas kernels for 0% -> 0%
where the time goes in v1:
time: 437 us; the launch traced here: 432 us
  waiting for transfers between devices  298 us (68%)
  matrix products  47.5 us (11%)
  local copies, waits for them, and re-layouts  33.9 us (8%)
  starting transfers between devices  30.5 us (7%)
  between operations  15 us (3%)
  other arithmetic  6.9 us (2%)
    all_gather x3, waiting for transfers between devices, per_device(): lax.all_gather(iterate.astype(jnp.bfloat16), 'col', axis=0, tiled=True)  99.8 us
    psum x1, waiting for transfers between devices, per_device(): hessian_panel = lax.psum(partial_panel, 'tok') / total_count  97.5 us
    all_gather x1, waiting for transfers between devices, per_device(): lax.all_gather(activations[:, :panel_width], 'col', axis=1, tiled=True)  47 us
    all_gather x1, waiting for transfers between devices, per_device(): diagonal_block = lax.all_gather(block_part, 'col', axis=0, tiled=True)  43.1 us
    ppermute x7, starting transfers between devices, per_device(): lax.ppermute(going_down, 'col', [(d, (d - 1) % ways) for d in range(ways)])  20.8 us
    dot_general x4, matrix products, per_device(): product = jnp.dot(iterate, damped, precision=highest)  19.6 us
    gather x1, local copies, waits for them, and re-layouts, per_device(): damping = 0.01 * jnp.mean(jnp.diagonal(diagonal_block))  17.7 us
    dot_general x4, matrix products, per_device(): iterate = 2.0 * iterate - jnp.dot(product, whole, precision=highest)  10.7 us
  transfers between devices with their start and end apart: 22, of which 13 were waited for; matrix products, arithmetic and copies ran while one was open for 6% of the time, Pallas kernels for 0%

profile of v1, /device:TPU:1, one launch (start us, length us, event | category | flops | bytes accessed | tf_op | source)
XLA Modules:
  0.0 432.1 jit_solution(5409084610778909414)
XLA Ops:
  8.6 47.0 %all-gather.9.cloned.1.call-done = bf16[2048,1024]{0,1:T(8,128)(2,1)} async-done(((bf16[2048,64]{0,1:T(8,128)(2,1)}), bf16[2048,1024]{0,1:T(8,128)(2,1)}) %all-gather.9.cloned.1.call-update) | async-done | bytes 4194320 | tf_op jit(solution)/shard_map/all_gather | solution.py:19
  55.5 6.6 %fusion.25 = f32[512,1024]{1,0:T(8,128)} fusion(bf16[2048,512]{1,0:T(8,128)(2,1)} %param.3, bf16[2048,1024]{0,1:T(8,128)(2,1)} %all-gather.9.cloned.1.call-done), kind=kOutput, calls=%fused_computation.53 | convolution fusion | flops 2147483648 | bytes 8388608 | tf_op jit(solution)/shard_map/dot_general | solution.py:17
  62.2 97.5 %all-reduce.2.cloned.1.call-done = f32[512,1024]{1,0:T(8,128)} async-done(((f32[512,1024]{1,0:T(8,128)}), f32[512,1024]{1,0:T(8,128)}) %all-reduce.2.cloned.1.call-update) | async-done | bytes 2097168 | tf_op jit(solution)/shard_map/psum | solution.py:23
  162.4 43.1 %all-gather.11.cloned.1.call-done = f32[1024,1024]{1,0:T(8,128)} async-done(((f32[64,1024]{1,0:T(8,128)}), f32[1024,1024]{1,0:T(8,128)}) %all-gather.11.cloned.1.call-update) | async-done | bytes 4194320 | tf_op jit(solution)/shard_map/all_gather | solution.py:25
  205.5 17.7 %gather_fusion = f32[1024]{0:T(1024)S(1)} fusion(f32[1024,1024]{1,0:T(8,128)} %all-gather.11.cloned.1.call-done, s32[1024]{0:T(1024)S(1)} %bitcast.16), kind=kCustom, calls=%fused_computation | custom fusion | bytes 16384 | tf_op jit(solution)/shard_map/jit(diagonal)/cond/branch_0_fun/gather | solution.py:27
  224.4 3.9 multiply_reduce_fusion
  229.0 4.9 %fusion.9 = f32[64,1024]{1,0:T(8,128)S(1)} fusion(f32[1024,1024]{1,0:T(8,128)} %all-gather.11.cloned.1.call-done, f32[]{:T(128)S(6)} %mul_shard_map.3, f32[]{:T(128)S(6)} %sqrt.3, s32[64]{0:T(128)S(1)} %iota_add_fusion), kind=kOutput, calls=%fused_computation.14 | convolution fusion | flops 808583168 | bytes 4456712 | tf_op jit(solution)/shard_map/dot_general | solution.py:40
  235.9 4.9 %fusion.8 = f32[64,1024]{1,0:T(8,128)S(1)} fusion(f32[64,1024]{1,0:T(8,128)S(1)} %get-tuple-element.6, f32[1024,1024]{1,0:T(8,128)} %all-gather.11.cloned.1.call-done, f32[]{:T(128)S(6)} %mul_shard_map.3), kind=kOutput, calls=%fused_computation.13 | convolution fusion | flops 808452096 | bytes 4718596 | tf_op jit(solution)/shard_map/dot_general | solution.py:40
  240.8 33.5 %all-gather.13.cloned.1.call-done = bf16[1024,1024]{1,0:T(8,128)(2,1)} async-done(((bf16[64,1024]{1,0:T(8,128)(2,1)}), bf16[1024,1024]{1,0:T(8,128)(2,1)}) %all-gather.13.cloned.1.call-update) | async-done | bytes 2097168 | tf_op jit(solution)/shard_map/all_gather | solution.py:37
  274.3 3.5 fusion.23
  278.0 4.9 %fusion.7 = f32[64,1024]{1,0:T(8,128)S(1)} fusion(f32[64,1024]{1,0:T(8,128)S(1)} %get-tuple-element.8, f32[1024,1024]{1,0:T(8,128)} %all-gather.11.cloned.1.call-done, f32[]{:T(128)S(6)} %mul_shard_map.3), kind=kOutput, calls=%fused_computation.12 | convolution fusion | flops 808452096 | bytes 4718596 | tf_op jit(solution)/shard_map/dot_general | solution.py:40
  282.9 33.1 %all-gather.15.cloned.1.call-done = bf16[1024,1024]{1,0:T(8,128)(2,1)} async-done(((bf16[64,1024]{1,0:T(8,128)(2,1)}), bf16[1024,1024]{1,0:T(8,128)(2,1)}) %all-gather.15.cloned.1.call-update) | async-done | bytes 2097168 | tf_op jit(solution)/shard_map/all_gather | solution.py:37
  316.0 3.5 fusion.24
  319.5 4.9 %fusion.6 = f32[64,1024]{1,0:T(8,128)S(1)} fusion(f32[64,1024]{1,0:T(8,128)S(1)} %get-tuple-element.10, f32[1024,1024]{1,0:T(8,128)} %all-gather.11.cloned.1.call-done, f32[]{:T(128)S(6)} %mul_shard_map.3), kind=kOutput, calls=%fused_computation.11 | convolution fusion | flops 808452096 | bytes 4718596 | tf_op jit(solution)/shard_map/dot_general | solution.py:40
  324.4 33.2 %all-gather.17.cloned.1.call-done = bf16[1024,1024]{1,0:T(8,128)(2,1)} async-done(((bf16[64,1024]{1,0:T(8,128)(2,1)}), bf16[1024,1024]{1,0:T(8,128)(2,1)}) %all-gather.17.cloned.1.call-update) | async-done | bytes 2097168 | tf_op jit(solution)/shard_map/all_gather | solution.py:37
  357.6 2.5 broadcast_in_dim.14
  362.8 3.3 collective-permute-done
  381.2 3.0 collective-permute-start.7
  387.4 4.4 %collective-permute-start.9 = (f32[64,1024]{1,0:T(8,128)S(1)}, f32[64,1024]{1,0:T(8,128)S(1)}, u32[]{:S(2)}, u32[]{:S(2)}) collective-permute-start(f32[64,1024]{1,0:T(8,128)S(1)} %collective-permute-done.7), channel_id=1, source_target_pairs={{0,15},{1,0},{2,1},{3,2},{4,3},{5,4},{6,5},{7,6},{8,7},{9,8},{10,9... | collective-permute-start | bytes 786440 | tf_op jit(solution)/shard_map/ppermute | solution.py:52
  394.3 5.2 %collective-permute-start.11 = (f32[64,1024]{1,0:T(8,128)S(1)}, f32[64,1024]{1,0:T(8,128)S(1)}, u32[]{:S(2)}, u32[]{:S(2)}) collective-permute-start(f32[64,1024]{1,0:T(8,128)S(1)} %collective-permute-done.9), channel_id=1, source_target_pairs={{0,15},{1,0},{2,1},{3,2},{4,3},{5,4},{6,5},{7,6},{8,7},{9,8},{10,9... | collective-permute-start | bytes 786440 | tf_op jit(solution)/shard_map/ppermute | solution.py:52
  401.6 5.5 %collective-permute-start.13 = (f32[64,1024]{1,0:T(8,128)S(1)}, f32[64,1024]{1,0:T(8,128)S(1)}, u32[]{:S(2)}, u32[]{:S(2)}) collective-permute-start(f32[64,1024]{1,0:T(8,128)S(1)} %collective-permute-done.11), channel_id=1, source_target_pairs={{0,15},{1,0},{2,1},{3,2},{4,3},{5,4},{6,5},{7,6},{8,7},{9,8},{10,9... | collective-permute-start | bytes 786440 | tf_op jit(solution)/shard_map/ppermute | solution.py:52
  410.0 3.9 collective-permute-done.14
  414.6 6.1 %fusion.26 = f32[512,1024]{1,0:T(8,128)S(1)} fusion(bf16[512,1024]{0,1:T(8,128)(2,1)} %all-gather.7.cloned.1.call-done, f32[1024,1024]{1,0:T(8,128)} %constant_dynamic-update-slice_fusion), kind=kOutput, calls=%fused_computation.54 | convolution fusion | flops 6442450944 | bytes 7340032 | tf_op jit(solution)/shard_map/dot_general | solution.py:61
  420.7 4.5 %fusion.5 = bf16[512,512]{1,0:T(8,128)(2,1)} fusion(f32[512,1024]{1,0:T(8,128)S(1)} %fusion.26, bf16[512,512]{1,0:T(8,128)(2,1)S(1)} %copy-done.3, s32[512,512]{1,0:T(8,128)S(1)} %copy-done.2, f32[512,1024]{1,0:T(8,128)S(1)} %copy-done), kind=kOutput, calls=%fused_computation.10 | convolution fusion | flops 3223060480 | bytes 6291456 | tf_op jit(solution)/shard_map/dot_general | solution.py:62
  (78 shorter events, 36.7 us)
Async XLA Ops:
  6.5 49.0 %all-gather.9.cloned.1.call-start = ((), (), s32[]{:S(2)}) async-start(), calls=%async_computation.1 | async-start | bytes 4456448 | tf_op jit(solution)/shard_map/all_gather | solution.py:19
  8.5 151.2 %all-reduce.2.cloned.1.call-start = ((), (), s32[]{:S(2)}) async-start(), calls=%async_computation.2 | async-start | bytes 4194304 | tf_op jit(solution)/shard_map/psum | solution.py:23
  62.2 143.3 %all-gather.11.cloned.1.call-start = ((), (), s32[]{:S(2)}) async-start(), calls=%async_computation.3 | async-start | bytes 4456448 | tf_op jit(solution)/shard_map/all_gather | solution.py:25
  162.3 112.0 %all-gather.13.cloned.1.call-start = ((), (), s32[]{:S(2)}) async-start(), calls=%async_computation.4 | async-start | bytes 2228224 | tf_op jit(solution)/shard_map/all_gather | solution.py:37
  235.8 80.1 %all-gather.15.cloned.1.call-start = ((), (), s32[]{:S(2)}) async-start(), calls=%async_computation.5 | async-start | bytes 2228224 | tf_op jit(solution)/shard_map/all_gather | solution.py:37
  277.8 79.9 %all-gather.17.cloned.1.call-start = ((), (), s32[]{:S(2)}) async-start(), calls=%async_computation.6 | async-start | bytes 2228224 | tf_op jit(solution)/shard_map/all_gather | solution.py:37
  319.4 95.2 %all-gather.7.cloned.1.call-start = ((), (), s32[]{:S(2)}) async-start(), calls=%async_computation | async-start | bytes 1114112 | tf_op jit(solution)/shard_map/all_gather | solution.py:60
  324.4 44.2 %slice-start = ((s32[512,512]{1,0:T(8,128)}), s32[512,64]{1,0:T(8,128)S(1)}, s32[]{:S(2)}) async-start(s32[512,512]{1,0:T(8,128)} %param.5), calls=%async_computation.7 | async-start | bytes 524288 | tf_op jit(solution)/shard_map/slice | solution.py:58
  324.4 44.3 %slice-start.1 = ((bf16[512,512]{1,0:T(8,128)(2,1)}), bf16[512,64]{1,0:T(8,128)(2,1)S(1)}, s32[]{:S(2)}) async-start(bf16[512,512]{1,0:T(8,128)(2,1)} %param.4), calls=%async_computation.8 | async-start | bytes 262144 | tf_op jit(solution)/shard_map/slice | solution.py:58
  362.1 4.0 collective-permute-start
  362.8 6.1 %collective-permute-start.1 = (f32[64,1024]{1,0:T(8,128)S(1)}, f32[64,1024]{1,0:T(8,128)S(1)}, u32[]{:S(2)}, u32[]{:S(2)}) collective-permute-start(f32[64,1024]{1,0:T(8,128)S(1)} %get-tuple-element.12), channel_id=1, source_target_pairs={{0,15},{1,0},{2,1},{3,2},{4,3},{5,4},{6,5},{7,6},{8,7},{9,8},{10,9... | collective-permute-start | bytes 786440 | tf_op jit(solution)/shard_map/ppermute | solution.py:52
  366.1 5.8 %collective-permute-start.2 = (f32[64,1024]{1,0:T(8,128)S(1)}, f32[64,1024]{1,0:T(8,128)S(1)}, u32[]{:S(2)}, u32[]{:S(2)}) collective-permute-start(f32[64,1024]{1,0:T(8,128)S(1)} %collective-permute-done), channel_id=1, source_target_pairs={{0,1},{1,2},{2,3},{3,4},{4,5},{5,6},{6,7},{7,8},{8,9},{9,10},{10,1... | collective-permute-start | bytes 786440 | tf_op jit(solution)/shard_map/ppermute | solution.py:49
  368.9 6.2 %collective-permute-start.3 = (f32[64,1024]{1,0:T(8,128)S(1)}, f32[64,1024]{1,0:T(8,128)S(1)}, u32[]{:S(2)}, u32[]{:S(2)}) collective-permute-start(f32[64,1024]{1,0:T(8,128)S(1)} %collective-permute-done.1), channel_id=1, source_target_pairs={{0,15},{1,0},{2,1},{3,2},{4,3},{5,4},{6,5},{7,6},{8,7},{9,8},{10,9... | collective-permute-start | bytes 786440 | tf_op jit(solution)/shard_map/ppermute | solution.py:52
  371.9 5.8 %collective-permute-start.4 = (f32[64,1024]{1,0:T(8,128)S(1)}, f32[64,1024]{1,0:T(8,128)S(1)}, u32[]{:S(2)}, u32[]{:S(2)}) collective-permute-start(f32[64,1024]{1,0:T(8,128)S(1)} %collective-permute-done.2), channel_id=1, source_target_pairs={{0,1},{1,2},{2,3},{3,4},{4,5},{5,6},{6,7},{7,8},{8,9},{9,10},{10,1... | collective-permute-start | bytes 786440 | tf_op jit(solution)/shard_map/ppermute | solution.py:49
  375.1 6.1 %collective-permute-start.5 = (f32[64,1024]{1,0:T(8,128)S(1)}, f32[64,1024]{1,0:T(8,128)S(1)}, u32[]{:S(2)}, u32[]{:S(2)}) collective-permute-start(f32[64,1024]{1,0:T(8,128)S(1)} %collective-permute-done.3), channel_id=1, source_target_pairs={{0,15},{1,0},{2,1},{3,2},{4,3},{5,4},{6,5},{7,6},{8,7},{9,8},{10,9... | collective-permute-start | bytes 786440 | tf_op jit(solution)/shard_map/ppermute | solution.py:52
  377.7 7.1 %collective-permute-start.6 = (f32[64,1024]{1,0:T(8,128)S(1)}, f32[64,1024]{1,0:T(8,128)S(1)}, u32[]{:S(2)}, u32[]{:S(2)}) collective-permute-start(f32[64,1024]{1,0:T(8,128)S(1)} %collective-permute-done.4), channel_id=1, source_target_pairs={{0,1},{1,2},{2,3},{3,4},{4,5},{5,6},{6,7},{7,8},{8,9},{9,10},{10,1... | collective-permute-start | bytes 786440 | tf_op jit(solution)/shard_map/ppermute | solution.py:49
  381.2 6.3 %collective-permute-start.7 = (f32[64,1024]{1,0:T(8,128)S(1)}, f32[64,1024]{1,0:T(8,128)S(1)}, u32[]{:S(2)}, u32[]{:S(2)}) collective-permute-start(f32[64,1024]{1,0:T(8,128)S(1)} %collective-permute-done.5), channel_id=1, source_target_pairs={{0,15},{1,0},{2,1},{3,2},{4,3},{5,4},{6,5},{7,6},{8,7},{9,8},{10,9... | collective-permute-start | bytes 786440 | tf_op jit(solution)/shard_map/ppermute | solution.py:52
  384.8 7.7 %collective-permute-start.8 = (f32[64,1024]{1,0:T(8,128)S(1)}, f32[64,1024]{1,0:T(8,128)S(1)}, u32[]{:S(2)}, u32[]{:S(2)}) collective-permute-start(f32[64,1024]{1,0:T(8,128)S(1)} %collective-permute-done.6), channel_id=1, source_target_pairs={{0,1},{1,2},{2,3},{3,4},{4,5},{5,6},{6,7},{7,8},{8,9},{9,10},{10,1... | collective-permute-start | bytes 786440 | tf_op jit(solution)/shard_map/ppermute | solution.py:49
  387.4 6.9 %collective-permute-start.9 = (f32[64,1024]{1,0:T(8,128)S(1)}, f32[64,1024]{1,0:T(8,128)S(1)}, u32[]{:S(2)}, u32[]{:S(2)}) collective-permute-start(f32[64,1024]{1,0:T(8,128)S(1)} %collective-permute-done.7), channel_id=1, source_target_pairs={{0,15},{1,0},{2,1},{3,2},{4,3},{5,4},{6,5},{7,6},{8,7},{9,8},{10,9... | collective-permute-start | bytes 786440 | tf_op jit(solution)/shard_map/ppermute | solution.py:52
  392.6 7.7 %collective-permute-start.10 = (f32[64,1024]{1,0:T(8,128)S(1)}, f32[64,1024]{1,0:T(8,128)S(1)}, u32[]{:S(2)}, u32[]{:S(2)}) collective-permute-start(f32[64,1024]{1,0:T(8,128)S(1)} %collective-permute-done.8), channel_id=1, source_target_pairs={{0,1},{1,2},{2,3},{3,4},{4,5},{5,6},{6,7},{7,8},{8,9},{9,10},{10,1... | collective-permute-start | bytes 786440 | tf_op jit(solution)/shard_map/ppermute | solution.py:49
  394.3 7.3 %collective-permute-start.11 = (f32[64,1024]{1,0:T(8,128)S(1)}, f32[64,1024]{1,0:T(8,128)S(1)}, u32[]{:S(2)}, u32[]{:S(2)}) collective-permute-start(f32[64,1024]{1,0:T(8,128)S(1)} %collective-permute-done.9), channel_id=1, source_target_pairs={{0,15},{1,0},{2,1},{3,2},{4,3},{5,4},{6,5},{7,6},{8,7},{9,8},{10,9... | collective-permute-start | bytes 786440 | tf_op jit(solution)/shard_map/ppermute | solution.py:52
  400.2 7.6 %collective-permute-start.12 = (f32[64,1024]{1,0:T(8,128)S(1)}, f32[64,1024]{1,0:T(8,128)S(1)}, u32[]{:S(2)}, u32[]{:S(2)}) collective-permute-start(f32[64,1024]{1,0:T(8,128)S(1)} %collective-permute-done.10), channel_id=1, source_target_pairs={{0,1},{1,2},{2,3},{3,4},{4,5},{5,6},{6,7},{7,8},{8,9},{9,10},{10,1... | collective-permute-start | bytes 786440 | tf_op jit(solution)/shard_map/ppermute | solution.py:49
  401.6 7.6 %collective-permute-start.13 = (f32[64,1024]{1,0:T(8,128)S(1)}, f32[64,1024]{1,0:T(8,128)S(1)}, u32[]{:S(2)}, u32[]{:S(2)}) collective-permute-start(f32[64,1024]{1,0:T(8,128)S(1)} %collective-permute-done.11), channel_id=1, source_target_pairs={{0,15},{1,0},{2,1},{3,2},{4,3},{5,4},{6,5},{7,6},{8,7},{9,8},{10,9... | collective-permute-start | bytes 786440 | tf_op jit(solution)/shard_map/ppermute | solution.py:52
  407.8 6.1 %collective-permute-start.14 = (f32[64,1024]{1,0:T(8,128)S(1)}, f32[64,1024]{1,0:T(8,128)S(1)}, u32[]{:S(2)}, u32[]{:S(2)}) collective-permute-start(f32[64,1024]{1,0:T(8,128)S(1)} %collective-permute-done.12), channel_id=1, source_target_pairs={{0,1},{1,2},{2,3},{3,4},{4,5},{5,6},{6,7},{7,8},{8,9},{9,10},{10,1... | collective-permute-start | bytes 786440 | tf_op jit(solution)/shard_map/ppermute | solution.py:49
  (4 other events, 31.5 us)
Sparse Core Ops, SparseCore 0:
  9.2 46.3 all-gather.8
  62.3 97.4 all-reduce.1
  162.4 43.0 all-gather.10
  235.9 38.2 all-gather.12
  277.9 38.0 all-gather.14
  319.6 38.0 all-gather.16
  375.2 39.1 all-gather.6
